TPU v7x, 32 devices: a whole 2x2x4 slice. The times are simulated.
32 devices in a mesh: seq: 8 (over y, x, core), tp: 4 (over z).
Axes of the slice: x: 2, y: 2, z: 4, core: 2. Of those that a mesh axis runs over, the one named last changes fastest.
Arguments:
- gate_input: bfloat16 [8192, 8192], P('seq', 'tp'), may hold values from -6 to 6
- key_input: bfloat16 [8192, 8192], P('seq', 'tp'), may hold values from -6 to 6
- value_input: bfloat16 [8192, 8192], P('seq', 'tp'), may hold values from -6 to 6
- filter_taps: bfloat16 [512, 2048], P('tp'), as said below
- out_weight: bfloat16 [4096, 8192], P(None, 'tp'), may hold values from -0.0625 to 0.0625
Outputs:
- mixed: bfloat16 [4096, 8192], P('tp', 'seq')
Inputs may be any that keep to these rules, and one draw needn't show every extreme that they name: `filter_taps`: one causal filter for each group of 16 consecutive channels, indexed by lag.
All inputs are finite; a program needn't handle non-finite values.
Results may differ from a plain program's by a relative error of at most 0.0095.
Values may be sent and summed in bfloat16 or wider, within the bound.
A program may use at most 192 MiB of HBM per device.

v0:
```python
import math

import jax
import jax.numpy as jnp
from jax import lax
from jax.sharding import PartitionSpec as P

GROUP_SIZE = 16
BLOCK = 128
SPAN = 2


def shifted(value, axis, steps):
    count = lax.axis_size(axis)
    leading, last = (max(0, -steps), min(count, count - steps))
    return lax.ppermute(value, axis, [(source, source + steps) for source in range(leading, last)])


def toeplitz_band(taps):
    batch_size, taps_length = taps.shape
    line_length = taps_length + 2 * BLOCK + 1
    leading = jnp.zeros((batch_size, BLOCK + 1), taps.dtype)
    trailing = jnp.zeros((batch_size, BLOCK), taps.dtype)
    line = jnp.concatenate([leading, taps[:, ::-1], trailing], axis=1)
    tiled = jnp.tile(line, (1, BLOCK))[:, : BLOCK * (line_length - 1)]
    tiled = tiled.reshape(batch_size, BLOCK, line_length - 1)
    return tiled[:, :, BLOCK : taps_length + 2 * BLOCK]


def convolve_batch(operands):
    taps, window = operands
    batch_size = taps.shape[0]
    lag_blocks = taps.shape[1] // BLOCK + 1
    out_blocks = window.shape[1] - lag_blocks + 1
    matrix = toeplitz_band(taps)
    columns = jnp.stack(
        [
            window[:, first : first + lag_blocks].reshape(
                batch_size, lag_blocks * BLOCK, GROUP_SIZE
            )
            for first in range(out_blocks)
        ],
        axis=2,
    )
    columns = columns.reshape(batch_size, lag_blocks * BLOCK, out_blocks * GROUP_SIZE)
    return jnp.einsum("gim,gmn->gin", matrix, columns, preferred_element_type=jnp.float32)


def group_blocks(product):
    tokens_here, width = product.shape
    grouped = product.reshape(
        tokens_here // BLOCK, BLOCK, width // GROUP_SIZE, GROUP_SIZE
    ).transpose(2, 0, 1, 3)
    return grouped.reshape(width // GROUP_SIZE, tokens_here // BLOCK, BLOCK * GROUP_SIZE)


def local_conv(extended, filter_taps, tokens_here, width):
    local_groups = width // GROUP_SIZE
    blocks_here = tokens_here // BLOCK
    window_count = extended.shape[1]
    batch_size = math.gcd(local_groups, 8)
    batches = local_groups // batch_size
    result = lax.map(
        convolve_batch,
        (
            filter_taps.reshape(batches, batch_size, filter_taps.shape[1]),
            extended.reshape(batches, batch_size, window_count, BLOCK * GROUP_SIZE),
        ),
    )
    result = result.reshape(batches, batch_size, BLOCK, blocks_here, GROUP_SIZE).transpose(
        3, 2, 0, 1, 4
    )
    return result.reshape(tokens_here, width)


def body(gate_input, key_input, value_input, filter_taps, out_weight):
    tokens_here, width = gate_input.shape
    product = (key_input.astype(jnp.float32) * value_input.astype(jnp.float32)).astype(jnp.bfloat16)
    grouped = group_blocks(product)
    earlier = []
    moving = grouped
    for passes in range(SPAN):
        moving = shifted(moving, "seq", 1)
        earlier.insert(0, moving)
    extended = jnp.concatenate(earlier + [grouped], axis=1)
    conv = local_conv(extended, filter_taps, tokens_here, width)
    gated = (gate_input.astype(jnp.float32) * conv).astype(jnp.bfloat16)
    return lax.psum_scatter(
        lax.dot_general(
            out_weight, gated, (((1,), (1,)), ((), ())), preferred_element_type=jnp.float32
        ).astype(jnp.bfloat16),
        "tp",
        scatter_dimension=0,
        tiled=True,
    )


def solution(mesh):
    return jax.shard_map(
        body,
        mesh=mesh,
        in_specs=(P("seq", "tp"), P("seq", "tp"), P("seq", "tp"), P("tp", None), P(None, "tp")),
        out_specs=P("tp", "seq"),
        check_vma=False,
    )
```

profile of v0, /device:TPU:10, one launch (start us, length us, event | category | flops | bytes accessed | tf_op | source)
XLA Modules:
  0.0 2373.8 jit_solution(6520798648652755717)
XLA Ops:
  6.5 7.7 multiply_convert_fusion
  14.3 6.4 copy.41
  26.0 12.2 copy.42
  40.2 48.2 %collective-permute-done = bf16[128,8,2048]{0,2,1:T(8,128)(2,1)} collective-permute-done((bf16[128,8,2048]{0,2,1:T(8,128)(2,1)}, bf16[128,8,2048]{0,2,1:T(8,128)(2,1)}, u32[]{:S(2)}, u32[]{:S(2)}) %collective-permute-start) | collective-permute-done | bytes 4194336 | tf_op jit(solution)/shard_map/ppermute | solution.py:16
  90.3 23.7 copy.45
  113.9 57.6 %concatenate.15 = bf16[16,8,8,2048]{3,2,1,0:T(8,128)(2,1)} reshape(bf16[128,8,128,16]{3,2,1,0:T(8,128)(2,1)} %copy.45) | data formatting | bytes 8388608 | tf_op jit(solution)/shard_map/concatenate | solution.py:85
  171.5 6.4 copy.40
  177.9 6.7 copy.44
  184.7 6.7 copy.43
  191.4 9.6 pad_maximum_fusion
  201.0 1983.1 %while.10 = (s32[]{:T(128)}, f32[16,8,128,128]{2,3,1,0:T(8,128)}, bf16[16,8,2048]{2,1,0:T(8,128)(2,1)}, bf16[16,8,24,2048]{3,2,1,0:T(8,128)(2,1)}, s32[]{:T(128)}, /*index=5*/bf16[]{:T(256)}) while((s32[]{:T(128)}, f32[16,8,128,128]{2,3,1,0:T(8,128)}, bf16[16,8,2048]{2,1,0:T(8,128)(2,1)}, bf16[16,8,24,2048]{3,2,1,0:T(8,128)(2,1)}, s32[]{:T(128)}, ...), condition=%wide.region_1.2_spmd, body=%wide.region_0.1_spmd.sunk | while | flops 570425344 | bytes 107473624 | solution.py:63
  222.4 5.8 reshape.70
  312.7 13.1 reshape.78
  325.8 9.5 tile.12
  345.2 5.8 reshape.70
  369.7 5.8 reshape.72
  382.0 5.8 reshape.73
  435.6 13.1 reshape.78
  448.6 9.5 tile.12
  468.1 5.8 reshape.70
  558.4 13.1 reshape.78
  571.5 9.5 tile.12
  590.9 5.8 reshape.70
  681.3 13.1 reshape.78
  694.4 9.5 tile.12
  713.8 5.8 reshape.70
  804.1 13.1 reshape.78
  817.2 9.5 tile.12
  836.6 5.8 reshape.70
  927.0 13.1 reshape.78
  940.1 9.5 tile.12
  959.5 5.8 reshape.70
  1049.8 13.1 reshape.78
  1062.9 9.5 tile.12
  1082.3 5.8 reshape.70
  1172.7 13.1 reshape.78
  1185.7 9.5 tile.12
  1205.1 5.8 reshape.70
  1295.5 13.1 reshape.78
  1308.5 9.5 tile.12
  1328.0 5.8 reshape.70
  1418.3 13.1 reshape.78
  1431.4 9.5 tile.12
  1450.8 5.8 reshape.70
  1541.2 13.1 reshape.78
  1554.2 9.5 tile.12
  1573.7 5.8 reshape.70
  1664.0 13.1 reshape.78
  1677.1 9.5 tile.12
  1696.5 5.8 reshape.70
  1786.8 13.1 reshape.78
  1799.9 9.5 tile.12
  1819.3 5.8 reshape.70
  1909.7 13.1 reshape.78
  1922.7 9.5 tile.12
  1942.1 5.8 reshape.70
  2032.5 13.1 reshape.78
  2045.5 9.5 tile.12
  2065.0 5.8 reshape.70
  2155.3 13.1 reshape.78
  2168.4 9.5 tile.12
  2184.1 7.7 copy.47
  2191.8 24.1 %convert_bitcast_fusion = bf16[4096,1024]{0,1:T(8,128)(2,1)} fusion(bf16[4096,2048]{1,0:T(8,128)(2,1)} %param.11, f32[256,8,8,128]{3,2,1,0:T(8,128)S(1)} %bitcast.65, bf16[1024,2048]{0,1:T(8,128)(2,1)S(1)} %copy-done), kind=kOutput, calls=%fused_computation.18 | convolution fusion | flops 17190354944 | bytes 37748736 | tf_op jit(solution)/shard_map/dot_general | solution.py:89
  2216.0 146.6 %reduce-scatter.2.cloned.1.call-done = bf16[1024,1024]{0,1:T(8,128)(2,1)} async-done(((bf16[4096,1024]{0,1:T(8,128)(2,1)}), bf16[1024,1024]{0,1:T(8,128)(2,1)}) %reduce-scatter.2.cloned.1.call-update) | async-done | bytes 2097168 | tf_op jit(solution)/shard_map/reduce_scatter | solution.py:88
  (648 shorter events, 1512.4 us)
Async XLA Ops:
  6.5 2356.1 %reduce-scatter.2.cloned.1.call-start = ((), (), s32[]{:S(2)}) async-start(), calls=%async_computation.1 | async-start | bytes 10485760 | tf_op jit(solution)/shard_map/reduce_scatter | solution.py:88
  38.2 50.1 %collective-permute-start = (bf16[128,8,2048]{0,2,1:T(8,128)(2,1)}, bf16[128,8,2048]{0,2,1:T(8,128)(2,1)}, u32[]{:S(2)}, u32[]{:S(2)}) collective-permute-start(bf16[128,8,2048]{0,2,1:T(8,128)(2,1)} %bitcast.66), channel_id=1, source_target_pairs={{0,4},{4,8},{8,12},{12,16},{16,20},{20,24},{24,28},{1,5},{5,9},{9,... | collective-permute-start | bytes 12582920 | tf_op jit(solution)/shard_map/ppermute | solution.py:16
  88.4 96.3 %collective-permute-start.1 = (bf16[128,8,2048]{0,2,1:T(8,128)(2,1)}, bf16[128,8,2048]{0,2,1:T(8,128)(2,1)}, u32[]{:S(2)}, u32[]{:S(2)}) collective-permute-start(bf16[128,8,2048]{0,2,1:T(8,128)(2,1)} %collective-permute-done), channel_id=1, source_target_pairs={{0,4},{4,8},{8,12},{12,16},{16,20},{20,24},{24,28},{1,5},{5,9},{9,... | collective-permute-start | bytes 12582920 | tf_op jit(solution)/shard_map/ppermute | solution.py:16
  335.3 2.3 slice-start
  335.3 3.6 slice-start.1
  337.6 1.4 slice-start.2
  458.2 2.3 slice-start
  458.2 3.6 slice-start.1
  460.5 1.4 slice-start.2
  581.0 2.3 slice-start
  581.0 3.6 slice-start.1
  583.3 1.4 slice-start.2
  703.9 2.3 slice-start
  703.9 3.6 slice-start.1
  706.2 1.4 slice-start.2
  826.7 2.3 slice-start
  826.7 3.6 slice-start.1
  829.1 1.4 slice-start.2
  949.6 2.3 slice-start
  949.6 3.6 slice-start.1
  951.9 1.4 slice-start.2
  1072.4 2.3 slice-start
  1072.4 3.6 slice-start.1
  1074.7 1.4 slice-start.2
  1195.3 2.3 slice-start
  1195.3 3.6 slice-start.1
  1197.6 1.4 slice-start.2
  1318.1 2.3 slice-start
  1318.1 3.6 slice-start.1
  1320.4 1.4 slice-start.2
  1440.9 2.3 slice-start
  1440.9 3.6 slice-start.1
  1443.2 1.4 slice-start.2
  1563.7 2.3 slice-start
  1563.7 3.6 slice-start.1
  1566.1 1.4 slice-start.2
  1686.6 2.3 slice-start
  1686.6 3.6 slice-start.1
  1688.9 1.4 slice-start.2
  1809.4 2.3 slice-start
  1809.4 3.6 slice-start.1
  1811.7 1.4 slice-start.2
  1932.3 2.3 slice-start
  1932.3 3.6 slice-start.1
  1934.6 1.4 slice-start.2
  2055.1 2.3 slice-start
  2055.1 3.6 slice-start.1
  2057.4 1.4 slice-start.2
  2177.9 2.3 slice-start
  2177.9 3.6 slice-start.1
  2180.2 1.4 slice-start.2
  2184.1 7.7 copy-start
Sparse Core Ops, SparseCore 0:
  2216.1 146.4 reduce-scatter.1
where the time goes:
time: 2400 us; the launch traced here: 2370 us
  local copies, waits for them, and re-layouts  2070 us (86%)
  waiting for transfers between devices  195 us (8%)
  matrix products  60 us (2%)
    reshape x256, local copies, waits for them, and re-layouts, convolve_batch(): jnp.stack([window[:, first:first + lag_blocks].reshape(batch_size, lag_bl...  1190 us
    while x208, local copies, waits for them, and re-layouts  397 us
    another operation x32, local copies, waits for them, and re-layouts, toeplitz_band(): tiled = jnp.tile(line, (1, BLOCK))[:, :BLOCK * (line_length - 1)]  192 us
    reduce_scatter x1, waiting for transfers between devices, body(): lax.psum_scatter(lax.dot_general(out_weight, gated, (((1,), (1,)), ((), (...  147 us
    concatenate x1, local copies, waits for them, and re-layouts, body(): extended = jnp.concatenate(earlier + [grouped], axis=1)  57.6 us
    ppermute x2, waiting for transfers between devices, shifted(): lax.ppermute(value, axis, [(source, source + steps) for source in range(l...  48.2 us
  transfers between devices with their start and end apart: 3, of which 2 were waited for; matrix products, arithmetic and copies ran while one was open for 4% of the time, Pallas kernels for 0%

commit v1 on v0

v1 whole, which is shorter than its diff:
```python
import functools
import math

import jax
import jax.numpy as jnp
from jax import lax
from jax.experimental import pallas as pl
from jax.experimental.pallas import tpu as pltpu
from jax.sharding import PartitionSpec as P

GROUP_SIZE = 16
LANES = 128
BLOCK = 256
CHANNELS = 128
HALO_CHUNKS = 4
TOKEN_CHUNKS = 4


def shifted(value, axis, steps):
    count = lax.axis_size(axis)
    return lax.ppermute(value, axis, [(source, source + steps) for source in range(count - steps)])


def product_kernel(key_ref, value_ref, out_ref):
    product = key_ref[...].astype(jnp.float32) * value_ref[...].astype(jnp.float32)
    out_ref[...] = product.T.astype(jnp.bfloat16)


def product_chunk(key_input, value_input, first, rows):
    tokens_here = key_input.shape[0]
    start = first // CHANNELS
    spec = pl.BlockSpec((tokens_here, CHANNELS), lambda i: (0, start + i))
    return pl.pallas_call(
        product_kernel,
        grid=(rows // CHANNELS,),
        in_specs=[spec, spec],
        out_specs=pl.BlockSpec((CHANNELS, tokens_here), lambda i: (i, 0)),
        out_shape=jax.ShapeDtypeStruct((rows, tokens_here), jnp.bfloat16),
        cost_estimate=pl.CostEstimate(
            flops=rows * tokens_here, bytes_accessed=6 * rows * tokens_here, transcendentals=0
        ),
    )(key_input, value_input)


def conv_kernel(span, taps_length, with_alias, gate_ref, taps_ref, *refs):
    sources = refs[: span + 1]
    out_ref, gate_t, lines = refs[span + 1 + (1 if with_alias else 0) :]
    tokens_here = out_ref.shape[1]
    gate_t[...] = gate_ref[...].astype(jnp.float32).T
    lines[:, :taps_length] = taps_ref[...].astype(jnp.float32)
    lines[:, taps_length:] = jnp.zeros((lines.shape[0], LANES), jnp.float32)
    per_block = BLOCK // LANES
    lag_tiles = taps_length // LANES
    lag_blocks = lag_tiles + per_block
    out_blocks = tokens_here // BLOCK
    per_source = tokens_here // LANES
    first_tile = (span + 1) * per_source - per_source - lag_tiles
    zeros = jnp.zeros((LANES, LANES), jnp.bfloat16)

    def one_group(group):
        rows = pl.ds(pl.multiple_of(group * GROUP_SIZE, GROUP_SIZE), GROUP_SIZE)
        tiles = []
        for index in range(first_tile, (span + 1) * per_source):
            source, place = divmod(index, per_source)
            tiles.append(sources[source][rows, place * LANES : (place + 1) * LANES])
        signal = jnp.concatenate(
            [
                jnp.concatenate(
                    [tiles[block * per_block + lag] for block in range(out_blocks)], axis=0
                )
                for lag in range(lag_blocks)
            ],
            axis=1,
        )
        line = lines[pl.ds(group, 1), :]
        spread = jnp.broadcast_to(line, (LANES, line.shape[1]))
        band = pltpu.roll(spread, 0, 1, stride=1, stride_axis=0).astype(jnp.bfloat16)

        def tile(index):
            if index < 0 or index > lag_tiles:
                return zeros
            return band[:, index * LANES : (index + 1) * LANES]

        matrix = jnp.concatenate(
            [
                jnp.concatenate(
                    [tile(lag_tiles + across - lag) for across in range(per_block)], axis=1
                )
                for lag in range(lag_blocks)
            ],
            axis=0,
        )
        conv = jnp.dot(signal, matrix, preferred_element_type=jnp.float32)
        for block in range(out_blocks):
            part = conv[block * GROUP_SIZE : (block + 1) * GROUP_SIZE]
            columns = slice(block * BLOCK, (block + 1) * BLOCK)
            out_ref[rows, columns] = (gate_t[rows, columns] * part).astype(jnp.bfloat16)

    def pair(step, carry):
        one_group(2 * step)
        one_group(2 * step + 1)
        return carry

    lax.fori_loop(0, CHANNELS // GROUP_SIZE // 2, pair, 0)


def conv_chunk(gate_input, filter_taps, sources, gated, first):
    tokens_here, width = gate_input.shape
    rows = sources[0].shape[0]
    taps_length = filter_taps.shape[1]
    start = first // CHANNELS
    groups = CHANNELS // GROUP_SIZE
    span = len(sources) - 1
    in_specs = [
        pl.BlockSpec((tokens_here, CHANNELS), lambda i: (0, start + i)),
        pl.BlockSpec((groups, taps_length), lambda i: (start + i, 0)),
    ] + [pl.BlockSpec((CHANNELS, tokens_here), lambda i: (i, 0))] * (span + 1)
    operands = [gate_input, filter_taps, *sources]
    aliases = {}
    if gated is not None:
        in_specs.append(pl.BlockSpec(memory_space=pl.ANY))
        aliases = {len(operands): 0}
        operands.append(gated)
    return pl.pallas_call(
        functools.partial(conv_kernel, span, taps_length, gated is not None),
        grid=(rows // CHANNELS,),
        in_specs=in_specs,
        out_specs=pl.BlockSpec((CHANNELS, tokens_here), lambda i: (start + i, 0)),
        out_shape=jax.ShapeDtypeStruct((width, tokens_here), jnp.bfloat16),
        scratch_shapes=[
            pltpu.VMEM((CHANNELS, tokens_here), jnp.float32),
            pltpu.VMEM((groups, taps_length + LANES), jnp.float32),
        ],
        input_output_aliases=aliases,
        compiler_params=pltpu.CompilerParams(vmem_limit_bytes=40 * 1024 * 1024),
        cost_estimate=pl.CostEstimate(
            flops=4 * rows * tokens_here * taps_length,
            bytes_accessed=2 * rows * tokens_here * (span + 3),
            transcendentals=0,
        ),
    )(*operands)


def body(gate_input, key_input, value_input, filter_taps, out_weight):
    tokens_here, width = gate_input.shape
    span = -(-filter_taps.shape[1] // tokens_here)
    chunks = math.gcd(width // CHANNELS, HALO_CHUNKS)
    rows = width // chunks
    moved = []
    for chunk in range(chunks):
        own = product_chunk(key_input, value_input, chunk * rows, rows)
        moved.append([own])
    for chunk in range(chunks):
        for _ in range(span):
            moved[chunk].insert(0, shifted(moved[chunk][0], "seq", 1))
    gated = None
    for chunk in range(chunks):
        gated = conv_chunk(gate_input, filter_taps, moved[chunk], gated, chunk * rows)
    pieces = []
    step = tokens_here // TOKEN_CHUNKS
    for chunk in range(TOKEN_CHUNKS):
        partial = lax.dot_general(
            out_weight,
            gated[:, chunk * step : (chunk + 1) * step],
            (((1,), (0,)), ((), ())),
            preferred_element_type=jnp.float32,
        ).astype(jnp.bfloat16)
        pieces.append(lax.psum_scatter(partial, "tp", scatter_dimension=0, tiled=True))
    return jnp.concatenate(pieces, axis=1)


def solution(mesh):
    return jax.shard_map(
        body,
        mesh=mesh,
        in_specs=(P("seq", "tp"), P("seq", "tp"), P("seq", "tp"), P("tp", None), P(None, "tp")),
        out_specs=P("tp", "seq"),
        check_vma=False,
    )
```

time: 2400 us -> 333 us (0.14)
  local copies, waits for them, and re-layouts: 2070 us -> 7.94 us
  Pallas kernels: 0 us -> 64.9 us
    reshape x256 -> x0, local copies, waits for them, and re-layouts: 1190 us -> none  [convolve_batch(): jnp.stack([window[:, first:first + lag_blocks].reshape(batch_size, lag_bl...]
    while x208 -> x0, local copies, waits for them, and re-layouts: 397 us -> none
    another operation x80 -> x0, local copies, waits for them, and re-layouts: 206 us -> none  [the longest x32 192 us: toeplitz_band(): tiled = jnp.tile(line, (1, BLOCK))[:, :BLOCK * (line_length - 1)]]
    slice x48 -> x0, local copies, waits for them, and re-layouts: 80.6 us -> none  [the longest x16 43.3 us: convolve_batch(): window[:, first:first + lag_blocks]]
    pallas_call x0 -> x8, Pallas kernels: none -> 64.9 us  [the longest x4 49.5 us: conv_chunk(): pl.pallas_call(functools.partial(conv_kernel, span, taps_length, gated is...]
    concatenate x17 -> x1, local copies, waits for them, and re-layouts: 59.2 us -> 2.56 us  [body(): return jnp.concatenate(pieces, axis=1)]
    transpose x3 -> x0, local copies, waits for them, and re-layouts: 43.6 us -> none  [the longest x2 35.9 us: group_blocks(): grouped = product.reshape(tokens_here // BLOCK, BLOCK, width // GROUP_SIZ...]
    squeeze x32 -> x0, local copies, waits for them, and re-layouts: 31.3 us -> none  [local_conv(): lax.map(convolve_batch, (filter_taps.reshape(batches, batch_size, filter_...]
  transfers between devices with their start and end apart: 3 -> 12, of which waited for: 2 -> 8; matrix products, arithmetic and copies ran while one was open for 4% -> 11% of each run, Pallas kernels for 0% -> 15%
where the time goes in v1:
time: 333 us; the launch traced here: 329 us
  waiting for transfers between devices  174 us (52%)
  Pallas kernels  64.9 us (19%)
  matrix products  48.3 us (15%)
  starting transfers between devices  19.1 us (6%)
  between operations  13.3 us (4%)
  local copies, waits for them, and re-layouts  7.94 us (2%)
    reduce_scatter x4, waiting for transfers between devices, body(): lax.psum_scatter(partial, 'tp', scatter_dimension=0, tiled=True)  142 us
    pallas_call x4, Pallas kernels, conv_chunk(): pl.pallas_call(functools.partial(conv_kernel, span, taps_length, gated is...  49.5 us
    dot_general x4, matrix products, body(): lax.dot_general(out_weight, gated[:, chunk * step:(chunk + 1) * step], ((...  48.3 us
    ppermute x8, waiting for transfers between devices, shifted(): lax.ppermute(value, axis, [(source, source + steps) for source in range(c...  31 us
    ppermute x8, starting transfers between devices, shifted(): lax.ppermute(value, axis, [(source, source + steps) for source in range(c...  18.6 us
    pallas_call x4, Pallas kernels, product_chunk(): pl.pallas_call(product_kernel, grid=(rows // CHANNELS,), in_specs=[spec,...  15.4 us
  transfers between devices with their start and end apart: 12, of which 8 were waited for; matrix products, arithmetic and copies ran while one was open for 11% of the time, Pallas kernels for 15%

profile of v1, /device:TPU:10, one launch (start us, length us, event | category | flops | bytes accessed | tf_op | source)
XLA Modules:
  0.0 328.9 jit_solution(15885307942530303100)
XLA Ops:
  6.5 0.0 reduce-scatter.11.cloned.1.call-start
  6.5 3.8 %shard_map.58.refs_2_ = bf16[512,1024]{1,0:T(8,128)(2,1)} custom-call(bf16[1024,2048]{1,0:T(8,128)(2,1)} %key_ref.7, bf16[1024,2048]{1,0:T(8,128)(2,1)} %value_ref.7), custom_call_target="tpu_custom_call" | custom-call | flops 524288 | bytes 3145728 | tf_op jit(solution)/shard_map/pallas_call | solution.py:33
  10.3 1.9 collective-permute-start.6
  12.2 3.9 %shard_map.57.refs_2_ = bf16[512,1024]{1,0:T(8,128)(2,1)} custom-call(bf16[1024,2048]{1,0:T(8,128)(2,1)} %key_ref.7, bf16[1024,2048]{1,0:T(8,128)(2,1)} %value_ref.7), custom_call_target="tpu_custom_call" | custom-call | flops 524288 | bytes 3145728 | tf_op jit(solution)/shard_map/pallas_call | solution.py:33
  16.1 3.5 %collective-permute-start.4 = (bf16[512,1024]{1,0:T(8,128)(2,1)}, bf16[512,1024]{1,0:T(8,128)(2,1)}, u32[]{:S(2)}, u32[]{:S(2)}) collective-permute-start(bf16[512,1024]{1,0:T(8,128)(2,1)} %shard_map.57.refs_2_), channel_id=1, source_target_pairs={{0,4},{4,8},{8,12},{12,16},{16,20},{20,24},{24,28},{1,5},{5,9},{9,... | collective-permute-start | bytes 3145736 | tf_op jit(solution)/shard_map/ppermute | solution.py:21
  19.6 3.8 %shard_map.56.refs_2_ = bf16[512,1024]{1,0:T(8,128)(2,1)} custom-call(bf16[1024,2048]{1,0:T(8,128)(2,1)} %key_ref.7, bf16[1024,2048]{1,0:T(8,128)(2,1)} %value_ref.7), custom_call_target="tpu_custom_call" | custom-call | flops 524288 | bytes 3145728 | tf_op jit(solution)/shard_map/pallas_call | solution.py:33
  23.4 0.0 copy-start.2
  23.4 2.0 collective-permute-start.2
  25.5 0.0 copy-start.5
  25.5 3.9 %shard_map.55.refs_2_ = bf16[512,1024]{1,0:T(8,128)(2,1)} custom-call(bf16[1024,2048]{1,0:T(8,128)(2,1)} %key_ref.7, bf16[1024,2048]{1,0:T(8,128)(2,1)} %value_ref.7), custom_call_target="tpu_custom_call" | custom-call | flops 524288 | bytes 3145728 | tf_op jit(solution)/shard_map/pallas_call | solution.py:33
  29.4 3.5 %collective-permute-start = (bf16[512,1024]{1,0:T(8,128)(2,1)}, bf16[512,1024]{1,0:T(8,128)(2,1)S(1)}, u32[]{:S(2)}, u32[]{:S(2)}) collective-permute-start(bf16[512,1024]{1,0:T(8,128)(2,1)} %shard_map.55.refs_2_), channel_id=1, source_target_pairs={{0,4},{4,8},{8,12},{12,16},{16,20},{20,24},{24,28},{1,5},{5,9},{9,... | collective-permute-start | bytes 3145736 | tf_op jit(solution)/shard_map/ppermute | solution.py:21
  32.9 0.0 collective-permute-done.6.refs_1_
  32.9 1.9 collective-permute-start.7
  34.8 3.1 collective-permute-done.4.refs_1_
  38.0 1.9 collective-permute-start.5
  39.9 9.2 %collective-permute-done.2.refs_1_ = bf16[512,1024]{1,0:T(8,128)(2,1)S(1)} collective-permute-done((bf16[512,1024]{1,0:T(8,128)(2,1)}, bf16[512,1024]{1,0:T(8,128)(2,1)S(1)}, u32[]{:S(2)}, u32[]{:S(2)}) %collective-permute-start.2) | collective-permute-done | bytes 1048608 | tf_op jit(solution)/shard_map/ppermute | solution.py:21
  49.1 1.9 collective-permute-start.3
  51.0 9.3 %collective-permute-done.refs_1_ = bf16[512,1024]{1,0:T(8,128)(2,1)S(1)} collective-permute-done((bf16[512,1024]{1,0:T(8,128)(2,1)}, bf16[512,1024]{1,0:T(8,128)(2,1)S(1)}, u32[]{:S(2)}, u32[]{:S(2)}) %collective-permute-start) | collective-permute-done | bytes 1048608 | tf_op jit(solution)/shard_map/ppermute | solution.py:21
  60.4 1.9 collective-permute-start.1
  62.3 9.3 %collective-permute-done.7.refs_0_ = bf16[512,1024]{1,0:T(8,128)(2,1)S(1)} collective-permute-done((bf16[512,1024]{1,0:T(8,128)(2,1)}, bf16[512,1024]{1,0:T(8,128)(2,1)S(1)}, u32[]{:S(2)}, u32[]{:S(2)}) %collective-permute-start.7) | collective-permute-done | bytes 1048608 | tf_op jit(solution)/shard_map/ppermute | solution.py:21
  71.6 0.0 copy-done.2
  71.6 0.0 copy-start
  71.6 2.2 copy-done
  73.8 0.0 copy-start.6
  73.8 1.2 copy-done.6
  75.0 12.8 %shard_map.59.refs_3_ = bf16[2048,1024]{1,0:T(8,128)(2,1)S(1)} custom-call(bf16[1024,2048]{1,0:T(8,128)(2,1)S(1)} %copy-done, bf16[128,2048]{1,0:T(8,128)(2,1)S(1)} %copy-done.2, bf16[512,1024]{1,0:T(8,128)(2,1)S(1)} %collective-permute-done.7.refs_0_, bf16[512,1024]{1,0:T(8,128)(2,1)} %collective-permute-done.6.refs_1_, bf16[512,1024]{1,0:T(8,128)(2,1)S(1)} %copy-done.6), custom_call_target="tpu_custom_call" | custom-call | flops 4294967296 | bytes 5242880 | tf_op jit(solution)/shard_map/pallas_call | solution.py:124
  87.8 0.0 copy-start.4
  87.8 0.0 collective-permute-done.5.refs_0_
  87.8 0.0 copy-done.5
  87.8 12.9 %shard_map.60.refs_3_ = bf16[2048,1024]{1,0:T(8,128)(2,1)S(1)} custom-call(bf16[1024,2048]{1,0:T(8,128)(2,1)S(1)} %copy-done, bf16[128,2048]{1,0:T(8,128)(2,1)S(1)} %copy-done.2, bf16[512,1024]{1,0:T(8,128)(2,1)S(1)} %collective-permute-done.5.refs_0_, bf16[512,1024]{1,0:T(8,128)(2,1)} %collective-permute-done.4.refs_1_, ...), custom_call_target="tpu_custom_call", output_to_operand_aliasing={{}: (5, {})} | custom-call | flops 4294967296 | bytes 5242880 | tf_op jit(solution)/shard_map/pallas_call | solution.py:124
  100.7 0.0 copy-start.3
  100.7 0.0 collective-permute-done.3.refs_0_
  100.8 0.0 copy-done.4
  100.8 11.9 %shard_map.61.refs_3_ = bf16[2048,1024]{1,0:T(8,128)(2,1)S(1)} custom-call(bf16[1024,2048]{1,0:T(8,128)(2,1)S(1)} %copy-done, bf16[128,2048]{1,0:T(8,128)(2,1)S(1)} %copy-done.2, bf16[512,1024]{1,0:T(8,128)(2,1)S(1)} %collective-permute-done.3.refs_0_, bf16[512,1024]{1,0:T(8,128)(2,1)S(1)} %collective-permute-done.2.refs_1_, ...), custom_call_target="tpu_custom_call", output_to_operand_aliasing={{}: (5, {})} | custom-call | flops 4294967296 | bytes 5242880 | tf_op jit(solution)/shard_map/pallas_call | solution.py:124
  112.7 0.0 collective-permute-done.1.refs_0_
  112.7 0.0 copy-done.3
  112.7 11.9 %shard_map.62 = bf16[2048,1024]{1,0:T(8,128)(2,1)S(1)} custom-call(bf16[1024,2048]{1,0:T(8,128)(2,1)S(1)} %copy-done, bf16[128,2048]{1,0:T(8,128)(2,1)S(1)} %copy-done.2, bf16[512,1024]{1,0:T(8,128)(2,1)S(1)} %collective-permute-done.1.refs_0_, bf16[512,1024]{1,0:T(8,128)(2,1)S(1)} %collective-permute-done.refs_1_, ...), custom_call_target="tpu_custom_call", output_to_operand_aliasing={{}: (5, {})} | custom-call | flops 4294967296 | bytes 5242880 | tf_op jit(solution)/shard_map/pallas_call | solution.py:124
  124.6 0.0 copy-start.1
  124.7 1.9 copy-done.1
  126.6 12.0 %fusion.3 = bf16[4096,256]{0,1:T(8,128)(2,1)} fusion(bf16[4096,2048]{1,0:T(8,128)(2,1)} %param.9, bf16[2048,1024]{1,0:T(8,128)(2,1)} %copy-done.1), kind=kOutput, calls=%fused_computation.7 | convolution fusion | flops 4296015872 | bytes 19922944 | tf_op jit(solution)/shard_map/dot_general | solution.py:162
  138.6 0.0 reduce-scatter.11.cloned.1.call-update
  138.6 0.2 reduce-scatter.5.cloned.1.call-start
  138.9 12.0 %fusion = bf16[4096,256]{0,1:T(8,128)(2,1)} fusion(bf16[4096,2048]{1,0:T(8,128)(2,1)} %param.9, bf16[2048,1024]{1,0:T(8,128)(2,1)} %copy-done.1), kind=kOutput, calls=%fused_computation.4 | convolution fusion | flops 4296015872 | bytes 19922944 | tf_op jit(solution)/shard_map/dot_general | solution.py:162
  150.9 0.0 reduce-scatter.5.cloned.1.call-update
  150.9 0.0 reduce-scatter.7.cloned.1.call-start
  151.0 12.1 %fusion.1 = bf16[4096,256]{0,1:T(8,128)(2,1)} fusion(bf16[4096,2048]{1,0:T(8,128)(2,1)} %param.9, bf16[2048,1024]{1,0:T(8,128)(2,1)} %copy-done.1), kind=kOutput, calls=%fused_computation.5 | convolution fusion | flops 4296015872 | bytes 19922944 | tf_op jit(solution)/shard_map/dot_general | solution.py:162
  163.1 0.0 reduce-scatter.7.cloned.1.call-update
  163.1 0.3 reduce-scatter.9.cloned.1.call-start
  163.4 12.2 %fusion.2 = bf16[4096,256]{0,1:T(8,128)(2,1)} fusion(bf16[4096,2048]{1,0:T(8,128)(2,1)} %param.9, bf16[2048,1024]{1,0:T(8,128)(2,1)} %copy-done.1), kind=kOutput, calls=%fused_computation.6 | convolution fusion | flops 4296015872 | bytes 19922944 | tf_op jit(solution)/shard_map/dot_general | solution.py:162
  175.6 0.0 reduce-scatter.9.cloned.1.call-update
  175.6 5.9 %reduce-scatter.11.cloned.1.call-done = bf16[1024,256]{0,1:T(8,128)(2,1)} async-done(((bf16[4096,256]{0,1:T(8,128)(2,1)}), bf16[1024,256]{0,1:T(8,128)(2,1)}) %reduce-scatter.11.cloned.1.call-update) | async-done | bytes 524304 | tf_op jit(solution)/shard_map/reduce_scatter | solution.py:168
  181.5 45.6 %reduce-scatter.5.cloned.1.call-done = bf16[1024,256]{0,1:T(8,128)(2,1)} async-done(((bf16[4096,256]{0,1:T(8,128)(2,1)}), bf16[1024,256]{0,1:T(8,128)(2,1)}) %reduce-scatter.5.cloned.1.call-update) | async-done | bytes 524304 | tf_op jit(solution)/shard_map/reduce_scatter | solution.py:168
  227.1 45.5 %reduce-scatter.7.cloned.1.call-done = bf16[1024,256]{0,1:T(8,128)(2,1)} async-done(((bf16[4096,256]{0,1:T(8,128)(2,1)}), bf16[1024,256]{0,1:T(8,128)(2,1)}) %reduce-scatter.7.cloned.1.call-update) | async-done | bytes 524304 | tf_op jit(solution)/shard_map/reduce_scatter | solution.py:168
  272.6 45.5 %reduce-scatter.9.cloned.1.call-done = bf16[1024,256]{0,1:T(8,128)(2,1)} async-done(((bf16[4096,256]{0,1:T(8,128)(2,1)}), bf16[1024,256]{0,1:T(8,128)(2,1)}) %reduce-scatter.9.cloned.1.call-update) | async-done | bytes 524304 | tf_op jit(solution)/shard_map/reduce_scatter | solution.py:168
  318.1 1.7 pad_maximum_fusion
  319.8 2.6 copy.9
Async XLA Ops:
  6.5 175.0 %reduce-scatter.11.cloned.1.call-start = ((), (), s32[]{:S(2)}) async-start(), calls=%async_computation.7 | async-start | bytes 2621440 | tf_op jit(solution)/shard_map/reduce_scatter | solution.py:168
  10.3 22.6 %collective-permute-start.6 = (bf16[512,1024]{1,0:T(8,128)(2,1)}, bf16[512,1024]{1,0:T(8,128)(2,1)}, u32[]{:S(2)}, u32[]{:S(2)}) collective-permute-start(bf16[512,1024]{1,0:T(8,128)(2,1)} %shard_map.58.refs_2_), channel_id=1, source_target_pairs={{0,4},{4,8},{8,12},{12,16},{16,20},{20,24},{24,28},{1,5},{5,9},{9,... | collective-permute-start | bytes 3145736 | tf_op jit(solution)/shard_map/ppermute | solution.py:21
  16.1 21.9 %collective-permute-start.4 = (bf16[512,1024]{1,0:T(8,128)(2,1)}, bf16[512,1024]{1,0:T(8,128)(2,1)}, u32[]{:S(2)}, u32[]{:S(2)}) collective-permute-start(bf16[512,1024]{1,0:T(8,128)(2,1)} %shard_map.57.refs_2_), channel_id=1, source_target_pairs={{0,4},{4,8},{8,12},{12,16},{16,20},{20,24},{24,28},{1,5},{5,9},{9,... | collective-permute-start | bytes 3145736 | tf_op jit(solution)/shard_map/ppermute | solution.py:21
  23.4 48.1 %copy-start.2 = (bf16[128,2048]{1,0:T(8,128)(2,1)S(1)}, bf16[128,2048]{1,0:T(8,128)(2,1)}, u32[]{:S(2)}) copy-start(bf16[128,2048]{1,0:T(8,128)(2,1)} %taps_ref.7) | copy-start | bytes 1572868
  23.4 25.7 %collective-permute-start.2 = (bf16[512,1024]{1,0:T(8,128)(2,1)}, bf16[512,1024]{1,0:T(8,128)(2,1)S(1)}, u32[]{:S(2)}, u32[]{:S(2)}) collective-permute-start(bf16[512,1024]{1,0:T(8,128)(2,1)} %shard_map.56.refs_2_), channel_id=1, source_target_pairs={{0,4},{4,8},{8,12},{12,16},{16,20},{20,24},{24,28},{1,5},{5,9},{9,... | collective-permute-start | bytes 3145736 | tf_op jit(solution)/shard_map/ppermute | solution.py:21
  25.5 62.3 %copy-start.5 = (bf16[512,1024]{1,0:T(8,128)(2,1)S(1)}, bf16[512,1024]{1,0:T(8,128)(2,1)}, u32[]{:S(2)}) copy-start(bf16[512,1024]{1,0:T(8,128)(2,1)} %shard_map.57.refs_2_) | copy-start | bytes 3145732
  29.4 30.9 %collective-permute-start = (bf16[512,1024]{1,0:T(8,128)(2,1)}, bf16[512,1024]{1,0:T(8,128)(2,1)S(1)}, u32[]{:S(2)}, u32[]{:S(2)}) collective-permute-start(bf16[512,1024]{1,0:T(8,128)(2,1)} %shard_map.55.refs_2_), channel_id=1, source_target_pairs={{0,4},{4,8},{8,12},{12,16},{16,20},{20,24},{24,28},{1,5},{5,9},{9,... | collective-permute-start | bytes 3145736 | tf_op jit(solution)/shard_map/ppermute | solution.py:21
  32.9 38.7 %collective-permute-start.7 = (bf16[512,1024]{1,0:T(8,128)(2,1)}, bf16[512,1024]{1,0:T(8,128)(2,1)S(1)}, u32[]{:S(2)}, u32[]{:S(2)}) collective-permute-start(bf16[512,1024]{1,0:T(8,128)(2,1)} %collective-permute-done.6.refs_1_), channel_id=1, source_target_pairs={{0,4},{4,8},{8,12},{12,16},{16,20},{20,24},{24,28},{1,5},{5,9},{9,... | collective-permute-start | bytes 3145736 | tf_op jit(solution)/shard_map/ppermute | solution.py:21
  38.0 49.8 %collective-permute-start.5 = (bf16[512,1024]{1,0:T(8,128)(2,1)}, bf16[512,1024]{1,0:T(8,128)(2,1)S(1)}, u32[]{:S(2)}, u32[]{:S(2)}) collective-permute-start(bf16[512,1024]{1,0:T(8,128)(2,1)} %collective-permute-done.4.refs_1_), channel_id=1, source_target_pairs={{0,4},{4,8},{8,12},{12,16},{16,20},{20,24},{24,28},{1,5},{5,9},{9,... | collective-permute-start | bytes 3145736 | tf_op jit(solution)/shard_map/ppermute | solution.py:21
  49.1 51.6 %collective-permute-start.3 = (bf16[512,1024]{1,0:T(8,128)(2,1)S(1)}, bf16[512,1024]{1,0:T(8,128)(2,1)S(1)}, u32[]{:S(2)}, u32[]{:S(2)}) collective-permute-start(bf16[512,1024]{1,0:T(8,128)(2,1)S(1)} %collective-permute-done.2.refs_1_), channel_id=1, source_target_pairs={{0,4},{4,8},{8,12},{12,16},{16,20},{20,24},{24,28},{1,5},{5,9},{9,... | collective-permute-start | bytes 3145736 | tf_op jit(solution)/shard_map/ppermute | solution.py:21
  60.4 52.3 %collective-permute-start.1 = (bf16[512,1024]{1,0:T(8,128)(2,1)S(1)}, bf16[512,1024]{1,0:T(8,128)(2,1)S(1)}, u32[]{:S(2)}, u32[]{:S(2)}) collective-permute-start(bf16[512,1024]{1,0:T(8,128)(2,1)S(1)} %collective-permute-done.refs_1_), channel_id=1, source_target_pairs={{0,4},{4,8},{8,12},{12,16},{16,20},{20,24},{24,28},{1,5},{5,9},{9,... | collective-permute-start | bytes 3145736 | tf_op jit(solution)/shard_map/ppermute | solution.py:21
  71.6 2.2 copy-start
  73.8 1.2 copy-start.6
  87.8 12.9 %copy-start.4 = (bf16[512,1024]{1,0:T(8,128)(2,1)S(1)}, bf16[512,1024]{1,0:T(8,128)(2,1)}, u32[]{:S(2)}) copy-start(bf16[512,1024]{1,0:T(8,128)(2,1)} %shard_map.56.refs_2_) | copy-start | bytes 3145732
  100.7 12.0 %copy-start.3 = (bf16[512,1024]{1,0:T(8,128)(2,1)S(1)}, bf16[512,1024]{1,0:T(8,128)(2,1)}, u32[]{:S(2)}) copy-start(bf16[512,1024]{1,0:T(8,128)(2,1)} %shard_map.55.refs_2_) | copy-start | bytes 3145732
  124.6 2.0 copy-start.1
  138.6 88.5 %reduce-scatter.5.cloned.1.call-start = ((), (), s32[]{:S(2)}) async-start(), calls=%async_computation.4 | async-start | bytes 2621440 | tf_op jit(solution)/shard_map/reduce_scatter | solution.py:168
  150.9 121.7 %reduce-scatter.7.cloned.1.call-start = ((), (), s32[]{:S(2)}) async-start(), calls=%async_computation.5 | async-start | bytes 2621440 | tf_op jit(solution)/shard_map/reduce_scatter | solution.py:168
  163.1 155.0 %reduce-scatter.9.cloned.1.call-start = ((), (), s32[]{:S(2)}) async-start(), calls=%async_computation.6 | async-start | bytes 2621440 | tf_op jit(solution)/shard_map/reduce_scatter | solution.py:168
Sparse Core Ops, SparseCore 0:
  138.8 42.7 reduce-scatter.10
  183.9 43.1 reduce-scatter.4
  229.4 43.1 reduce-scatter.6
  274.9 43.1 reduce-scatter.8

commit v2 on v1

--- a/solution.py
+++ b/solution.py
@@ -134,11 +134,43 @@
         input_output_aliases=aliases,
         compiler_params=pltpu.CompilerParams(vmem_limit_bytes=40 * 1024 * 1024),
         cost_estimate=pl.CostEstimate(
-            flops=4 * rows * tokens_here * taps_length,
+            flops=16 * rows * tokens_here * taps_length,
             bytes_accessed=2 * rows * tokens_here * (span + 3),
             transcendentals=0,
         ),
     )(*operands)
+
+
+def first_parts(partial, axis):
+    rows = partial.shape[0] // lax.axis_size(axis)
+    return partial[-rows:], partial[:rows]
+
+
+def scatter_sum(partial, ends, axis):
+    count = lax.axis_size(axis)
+    here = lax.axis_index(axis)
+    rows = partial.shape[0] // count
+
+    def part(index):
+        start = jnp.clip(index, 0, count - 1) * rows
+        return lax.dynamic_slice_in_dim(partial, start, rows, 0).astype(jnp.float32)
+
+    upward = downward = None
+    for step in range(1, count):
+        if step == 1:
+            up, down = ends
+        else:
+            up = part(count - step + here) + upward
+            down = part(here - count + step) + downward
+        upward = lax.ppermute(
+            up.astype(jnp.bfloat16), axis, [(source, source + 1) for source in range(step)]
+        ).astype(jnp.float32)
+        downward = lax.ppermute(
+            down.astype(jnp.bfloat16),
+            axis,
+            [(count - 1 - source, count - 2 - source) for source in range(step)],
+        ).astype(jnp.float32)
+    return (part(here) + upward + downward).astype(jnp.bfloat16)
 
 
 def body(gate_input, key_input, value_input, filter_taps, out_weight):
@@ -151,11 +183,17 @@
         own = product_chunk(key_input, value_input, chunk * rows, rows)
         moved.append([own])
     for chunk in range(chunks):
-        for _ in range(span):
-            moved[chunk].insert(0, shifted(moved[chunk][0], "seq", 1))
+        moved[chunk].insert(0, shifted(moved[chunk][0], "seq", 1))
     gated = None
     for chunk in range(chunks):
-        gated = conv_chunk(gate_input, filter_taps, moved[chunk], gated, chunk * rows)
+        for later in range(chunks) if chunk == 0 else []:
+            if later == chunks - 1 and later > 0:
+                gated = conv_chunk(gate_input, filter_taps, moved[0], None, 0)
+                moved[later][0], gated = lax.optimization_barrier((moved[later][0], gated))
+            for _ in range(span - 1):
+                moved[later].insert(0, shifted(moved[later][0], "seq", 1))
+        if chunk > 0 or gated is None:
+            gated = conv_chunk(gate_input, filter_taps, moved[chunk], gated, chunk * rows)
     pieces = []
     step = tokens_here // TOKEN_CHUNKS
     for chunk in range(TOKEN_CHUNKS):
@@ -165,7 +203,9 @@
             (((1,), (0,)), ((), ())),
             preferred_element_type=jnp.float32,
         ).astype(jnp.bfloat16)
-        pieces.append(lax.psum_scatter(partial, "tp", scatter_dimension=0, tiled=True))
+        ends = first_parts(partial, "tp")
+        gated, partial, ends = lax.optimization_barrier((gated, partial, ends))
+        pieces.append(scatter_sum(partial, ends, "tp"))
     return jnp.concatenate(pieces, axis=1)
 
 

time: 333 us -> 306 us (0.919)
  waiting for transfers between devices: 174 us -> 110 us
  starting transfers between devices: 19.1 us -> 63.1 us
  between operations: 13.3 us -> 0.72 us
  other arithmetic: 1.69 us -> 9.64 us
  local copies, waits for them, and re-layouts: 7.94 us -> 12.4 us
  matrix products: 48.3 us -> 44.1 us
    reduce_scatter x4 -> x0, waiting for transfers between devices: 142 us -> none  [body(): lax.psum_scatter(partial, 'tp', scatter_dimension=0, tiled=True)]
    ppermute x0 -> x24, waiting for transfers between devices: none -> 84.7 us  [the longest x12 52 us: scatter_sum(): lax.ppermute(down.astype(jnp.bfloat16), axis, [(count - 1 - source, count...]
    ppermute x0 -> x24, starting transfers between devices: none -> 43.5 us  [the longest x12 26.3 us: scatter_sum(): lax.ppermute(up.astype(jnp.bfloat16), axis, [(source, source + 1) for sou...]
    convert_element_type x0 -> x16, other arithmetic: none -> 9.47 us  [the longest x8 7.59 us: scatter_sum(): up.astype(jnp.bfloat16)]
    ppermute x8, waiting for transfers between devices: 31 us -> 25 us  [shifted(): lax.ppermute(value, axis, [(source, source + steps) for source in range(c...]
    slice x0 -> x4, local copies, waits for them, and re-layouts: none -> 4.64 us  [first_parts(): return (partial[-rows:], partial[:rows])]
    dot_general x4, matrix products: 48.3 us -> 44.1 us  [body(): lax.dot_general(out_weight, gated[:, chunk * step:(chunk + 1) * step], ((...]
  transfers between devices with their start and end apart: 12 -> 32, of which waited for: 8 -> 16; matrix products, arithmetic and copies ran while one was open for 11% -> 15% of each run, Pallas kernels for 15% -> 16%
where the time goes in v2:
time: 306 us; the launch traced here: 305 us
  waiting for transfers between devices  110 us (36%)
  Pallas kernels  65 us (21%)
  starting transfers between devices  63.1 us (21%)
  matrix products  44.1 us (14%)
  local copies, waits for them, and re-layouts  12.4 us (4%)
  other arithmetic  9.64 us (3%)
    ppermute x12, waiting for transfers between devices, scatter_sum(): lax.ppermute(down.astype(jnp.bfloat16), axis, [(count - 1 - source, count...  52 us
    pallas_call x4, Pallas kernels, conv_chunk(): pl.pallas_call(functools.partial(conv_kernel, span, taps_length, gated is...  49.7 us
    dot_general x4, matrix products, body(): lax.dot_general(out_weight, gated[:, chunk * step:(chunk + 1) * step], ((...  44.1 us
    ppermute x12, waiting for transfers between devices, scatter_sum(): lax.ppermute(up.astype(jnp.bfloat16), axis, [(source, source + 1) for sou...  32.8 us
    ppermute x12, starting transfers between devices, scatter_sum(): lax.ppermute(up.astype(jnp.bfloat16), axis, [(source, source + 1) for sou...  26.3 us
    ppermute x8, waiting for transfers between devices, shifted(): lax.ppermute(value, axis, [(source, source + steps) for source in range(c...  25 us
    ppermute x8, starting transfers between devices, shifted(): lax.ppermute(value, axis, [(source, source + steps) for source in range(c...  19.6 us
    ppermute x12, starting transfers between devices, scatter_sum(): lax.ppermute(down.astype(jnp.bfloat16), axis, [(count - 1 - source, count...  17.1 us
  transfers between devices with their start and end apart: 32, of which 16 were waited for; matrix products, arithmetic and copies ran while one was open for 15% of the time, Pallas kernels for 16%

profile of v2, /device:TPU:10, one launch (start us, length us, event | category | flops | bytes accessed | tf_op | source)
XLA Modules:
  0.0 304.7 jit_solution(425977875783995482)
XLA Ops:
  0.0 3.8 %shard_map.56.refs_2_ = bf16[512,1024]{1,0:T(8,128)(2,1)} custom-call(bf16[1024,2048]{1,0:T(8,128)(2,1)} %key_ref.7, bf16[1024,2048]{1,0:T(8,128)(2,1)} %value_ref.7), custom_call_target="tpu_custom_call" | custom-call | flops 524288 | bytes 3145728 | tf_op jit(solution)/shard_map/pallas_call | solution.py:33
  3.8 1.9 collective-permute-start.1
  5.7 3.8 %shard_map.59.refs_2_ = bf16[512,1024]{1,0:T(8,128)(2,1)} custom-call(bf16[1024,2048]{1,0:T(8,128)(2,1)} %key_ref.7, bf16[1024,2048]{1,0:T(8,128)(2,1)} %value_ref.7), custom_call_target="tpu_custom_call" | custom-call | flops 524288 | bytes 3145728 | tf_op jit(solution)/shard_map/pallas_call | solution.py:33
  9.5 3.5 %collective-permute-start.6 = (bf16[512,1024]{1,0:T(8,128)(2,1)}, bf16[512,1024]{1,0:T(8,128)(2,1)S(1)}, u32[]{:S(2)}, u32[]{:S(2)}) collective-permute-start(bf16[512,1024]{1,0:T(8,128)(2,1)} %shard_map.59.refs_2_), channel_id=1, source_target_pairs={{0,4},{4,8},{8,12},{12,16},{16,20},{20,24},{24,28},{1,5},{5,9},{9,... | collective-permute-start | bytes 3145736 | tf_op jit(solution)/shard_map/ppermute | solution.py:21
  13.0 3.8 %shard_map.58.refs_2_ = bf16[512,1024]{1,0:T(8,128)(2,1)} custom-call(bf16[1024,2048]{1,0:T(8,128)(2,1)} %key_ref.7, bf16[1024,2048]{1,0:T(8,128)(2,1)} %value_ref.7), custom_call_target="tpu_custom_call" | custom-call | flops 524288 | bytes 3145728 | tf_op jit(solution)/shard_map/pallas_call | solution.py:33
  16.9 2.0 collective-permute-start.4
  18.9 1.3 collective-permute-done.1.refs_1_
  20.2 2.2 collective-permute-start.2
  22.4 3.8 %shard_map.55.refs_2_ = bf16[512,1024]{1,0:T(8,128)(2,1)} custom-call(bf16[1024,2048]{1,0:T(8,128)(2,1)} %key_ref.7, bf16[1024,2048]{1,0:T(8,128)(2,1)} %value_ref.7), custom_call_target="tpu_custom_call" | custom-call | flops 524288 | bytes 3145728 | tf_op jit(solution)/shard_map/pallas_call | solution.py:33
  26.2 4.1 %collective-permute-start = (bf16[512,1024]{1,0:T(8,128)(2,1)}, bf16[512,1024]{1,0:T(8,128)(2,1)}, u32[]{:S(2)}, u32[]{:S(2)}) collective-permute-start(bf16[512,1024]{1,0:T(8,128)(2,1)} %shard_map.55.refs_2_), channel_id=1, source_target_pairs={{0,4},{4,8},{8,12},{12,16},{16,20},{20,24},{24,28},{1,5},{5,9},{9,... | collective-permute-start | bytes 3145736 | tf_op jit(solution)/shard_map/ppermute | solution.py:21
  31.4 1.9 collective-permute-start.7
  33.3 9.3 %collective-permute-done.4.refs_1_ = bf16[512,1024]{1,0:T(8,128)(2,1)S(1)} collective-permute-done((bf16[512,1024]{1,0:T(8,128)(2,1)}, bf16[512,1024]{1,0:T(8,128)(2,1)S(1)}, u32[]{:S(2)}, u32[]{:S(2)}) %collective-permute-start.4) | collective-permute-done | bytes 1048608 | tf_op jit(solution)/shard_map/ppermute | solution.py:21
  42.6 1.9 collective-permute-start.5
  44.5 9.4 %collective-permute-done.2.refs_0_ = bf16[512,1024]{1,0:T(8,128)(2,1)} collective-permute-done((bf16[512,1024]{1,0:T(8,128)(2,1)}, bf16[512,1024]{1,0:T(8,128)(2,1)}, u32[]{:S(2)}, u32[]{:S(2)}) %collective-permute-start.2) | collective-permute-done | bytes 1048608 | tf_op jit(solution)/shard_map/ppermute | solution.py:21
  53.9 2.2 copy-done.4
  57.2 13.1 %shard_map.57.refs_3_ = bf16[2048,1024]{1,0:T(8,128)(2,1)S(1)} custom-call(bf16[1024,2048]{1,0:T(8,128)(2,1)S(1)} %copy-done.4, bf16[128,2048]{1,0:T(8,128)(2,1)S(1)} %copy-done.6, bf16[512,1024]{1,0:T(8,128)(2,1)} %collective-permute-done.2.refs_0_, bf16[512,1024]{1,0:T(8,128)(2,1)} %collective-permute-done.1.refs_1_, bf16[512,1024]{1,0:T(8,128)(2,1)S(1)} %copy-done.3), custom_call_target="tpu_custom_call" | custom-call | flops 17179869184 | bytes 5242880 | tf_op jit(solution)/shard_map/pallas_call | solution.py:124
  70.3 2.1 collective-permute-start.3
  72.3 4.0 %collective-permute-done.7.refs_0_ = bf16[512,1024]{1,0:T(8,128)(2,1)S(1)} collective-permute-done((bf16[512,1024]{1,0:T(8,128)(2,1)S(1)}, bf16[512,1024]{1,0:T(8,128)(2,1)S(1)}, u32[]{:S(2)}, u32[]{:S(2)}) %collective-permute-start.7) | collective-permute-done | bytes 1048608 | tf_op jit(solution)/shard_map/ppermute | solution.py:21
  76.3 11.9 %shard_map.60.refs_3_ = bf16[2048,1024]{1,0:T(8,128)(2,1)S(1)} custom-call(bf16[1024,2048]{1,0:T(8,128)(2,1)S(1)} %copy-done.5, bf16[128,2048]{1,0:T(8,128)(2,1)S(1)} %copy-done.6, bf16[512,1024]{1,0:T(8,128)(2,1)S(1)} %collective-permute-done.7.refs_0_, bf16[512,1024]{1,0:T(8,128)(2,1)S(1)} %collective-permute-done.6.refs_1_, ...), custom_call_target="tpu_custom_call", output_to_operand_aliasing={{}: (5, {})} | custom-call | flops 17179869184 | bytes 5242880 | tf_op jit(solution)/shard_map/pallas_call | solution.py:124
  88.3 11.9 %shard_map.61.refs_3_ = bf16[2048,1024]{1,0:T(8,128)(2,1)S(1)} custom-call(bf16[1024,2048]{1,0:T(8,128)(2,1)S(1)} %copy-done.5, bf16[128,2048]{1,0:T(8,128)(2,1)S(1)} %copy-done.6, bf16[512,1024]{1,0:T(8,128)(2,1)S(1)} %collective-permute-done.5.refs_0_, bf16[512,1024]{1,0:T(8,128)(2,1)S(1)} %collective-permute-done.4.refs_1_, ...), custom_call_target="tpu_custom_call", output_to_operand_aliasing={{}: (5, {})} | custom-call | flops 17179869184 | bytes 5242880 | tf_op jit(solution)/shard_map/pallas_call | solution.py:124
  100.2 12.8 %shard_map.62 = bf16[2048,1024]{1,0:T(8,128)(2,1)S(1)} custom-call(bf16[1024,2048]{1,0:T(8,128)(2,1)S(1)} %copy-done.5, bf16[128,2048]{1,0:T(8,128)(2,1)S(1)} %copy-done.6, bf16[512,1024]{1,0:T(8,128)(2,1)S(1)} %collective-permute-done.3.refs_0_, bf16[512,1024]{1,0:T(8,128)(2,1)} %collective-permute-done.refs_1_, ...), custom_call_target="tpu_custom_call", output_to_operand_aliasing={{}: (5, {})} | custom-call | flops 17179869184 | bytes 5242880 | tf_op jit(solution)/shard_map/pallas_call | solution.py:124
  113.0 2.0 copy-done.7
  115.0 10.7 %fusion = bf16[4096,256]{0,1:T(8,128)(2,1)S(1)} fusion(bf16[4096,2048]{1,0:T(8,128)(2,1)} %param.9, bf16[2048,1024]{1,0:T(8,128)(2,1)} %copy-done.7), kind=kOutput, calls=%fused_computation.4 | convolution fusion | flops 4296015872 | bytes 19922944 | tf_op jit(solution)/shard_map/dot_general | solution.py:200
  126.8 1.3 collective-permute-start.8
  128.1 1.5 collective-permute-start.11
  129.6 10.7 %fusion.1 = bf16[4096,256]{0,1:T(8,128)(2,1)S(1)} fusion(bf16[4096,2048]{1,0:T(8,128)(2,1)} %param.9, bf16[2048,1024]{1,0:T(8,128)(2,1)} %copy-done.7), kind=kOutput, calls=%fused_computation.5 | convolution fusion | flops 4296015872 | bytes 19922944 | tf_op jit(solution)/shard_map/dot_general | solution.py:200
  141.5 1.3 collective-permute-start.14
  142.7 1.5 collective-permute-start.17
  144.2 12.0 %fusion.2 = bf16[4096,256]{0,1:T(8,128)(2,1)} fusion(bf16[4096,2048]{1,0:T(8,128)(2,1)} %param.9, bf16[2048,1024]{1,0:T(8,128)(2,1)} %copy-done.7), kind=kOutput, calls=%fused_computation.6 | convolution fusion | flops 4296015872 | bytes 19922944 | tf_op jit(solution)/shard_map/dot_general | solution.py:200
  156.2 2.3 fusion.9
  158.5 1.5 collective-permute-start.20
  160.0 10.7 %fusion.3 = bf16[4096,256]{0,1:T(8,128)(2,1)S(1)} fusion(bf16[4096,2048]{1,0:T(8,128)(2,1)} %param.9, bf16[2048,1024]{1,0:T(8,128)(2,1)} %copy-done.7), kind=kOutput, calls=%fused_computation.7 | convolution fusion | flops 4296015872 | bytes 19922944 | tf_op jit(solution)/shard_map/dot_general | solution.py:200
  170.9 1.6 collective-permute-start.26
  172.4 1.2 add_convert_fusion.19
  173.7 2.1 collective-permute-start.9
  179.0 9.5 %collective-permute-done.26 = bf16[1024,256]{0,1:T(8,128)(2,1)S(1)} collective-permute-done((bf16[1024,256]{0,1:T(8,128)(2,1)S(1)}, bf16[1024,256]{0,1:T(8,128)(2,1)S(1)}, u32[]{:S(2)}, u32[]{:S(2)}) %collective-permute-start.26) | collective-permute-done | bytes 524320 | tf_op jit(solution)/shard_map/ppermute | solution.py:165
  188.5 1.9 collective-permute-start.15
  191.4 8.4 %collective-permute-done.9 = bf16[1024,256]{0,1:T(8,128)(2,1)S(1)} collective-permute-done((bf16[1024,256]{0,1:T(8,128)(2,1)S(1)}, bf16[1024,256]{0,1:T(8,128)(2,1)S(1)}, u32[]{:S(2)}, u32[]{:S(2)}) %collective-permute-start.9) | collective-permute-done | bytes 524320 | tf_op jit(solution)/shard_map/ppermute | solution.py:165
  199.8 1.9 collective-permute-start.21
  201.7 1.4 add_convert_fusion.18
  203.1 1.9 collective-permute-start.27
  205.1 5.9 %collective-permute-done.15 = bf16[1024,256]{0,1:T(8,128)(2,1)S(1)} collective-permute-done((bf16[1024,256]{0,1:T(8,128)(2,1)S(1)}, bf16[1024,256]{0,1:T(8,128)(2,1)S(1)}, u32[]{:S(2)}, u32[]{:S(2)}) %collective-permute-start.15) | collective-permute-done | bytes 524320 | tf_op jit(solution)/shard_map/ppermute | solution.py:165
  211.0 1.3 collective-permute-start.12
  212.3 1.4 add_convert_fusion.13
  213.8 4.6 %collective-permute-start.10 = (bf16[1024,256]{0,1:T(8,128)(2,1)S(1)}, bf16[1024,256]{0,1:T(8,128)(2,1)S(1)}, u32[]{:S(2)}, u32[]{:S(2)}) collective-permute-start(bf16[1024,256]{0,1:T(8,128)(2,1)S(1)} %get-tuple-element.39), channel_id=1, source_target_pairs={{0,1},{1,2},{2,3},{4,5},{5,6},{6,7},{8,9},{9,10},{10,11},{12,13},{... | collective-permute-start | bytes 1572872 | tf_op jit(solution)/shard_map/ppermute | solution.py:165
  218.3 3.9 %collective-permute-done.21 = bf16[1024,256]{0,1:T(8,128)(2,1)S(1)} collective-permute-done((bf16[1024,256]{0,1:T(8,128)(2,1)S(1)}, bf16[1024,256]{0,1:T(8,128)(2,1)S(1)}, u32[]{:S(2)}, u32[]{:S(2)}) %collective-permute-start.21) | collective-permute-done | bytes 524320 | tf_op jit(solution)/shard_map/ppermute | solution.py:165
  222.2 1.3 collective-permute-start.18
  224.0 4.5 %collective-permute-start.16 = (bf16[1024,256]{0,1:T(8,128)(2,1)S(1)}, bf16[1024,256]{0,1:T(8,128)(2,1)S(1)}, u32[]{:S(2)}, u32[]{:S(2)}) collective-permute-start(bf16[1024,256]{0,1:T(8,128)(2,1)S(1)} %get-tuple-element.41), channel_id=1, source_target_pairs={{0,1},{1,2},{2,3},{4,5},{5,6},{6,7},{8,9},{9,10},{10,11},{12,13},{... | collective-permute-start | bytes 1572872 | tf_op jit(solution)/shard_map/ppermute | solution.py:165
  228.5 5.0 %collective-permute-done.27 = bf16[1024,256]{0,1:T(8,128)(2,1)S(1)} collective-permute-done((bf16[1024,256]{0,1:T(8,128)(2,1)S(1)}, bf16[1024,256]{0,1:T(8,128)(2,1)S(1)}, u32[]{:S(2)}, u32[]{:S(2)}) %collective-permute-start.27) | collective-permute-done | bytes 524320 | tf_op jit(solution)/shard_map/ppermute | solution.py:165
  233.5 1.3 collective-permute-start.24
  235.2 1.3 collective-permute-start.30
  236.7 1.9 collective-permute-start.13
  238.8 11.4 %collective-permute-done.24 = bf16[1024,256]{0,1:T(8,128)(2,1)S(1)} collective-permute-done((bf16[1024,256]{0,1:T(8,128)(2,1)S(1)}, bf16[1024,256]{0,1:T(8,128)(2,1)S(1)}, u32[]{:S(2)}, u32[]{:S(2)}) %collective-permute-start.24) | collective-permute-done | bytes 524320 | tf_op jit(solution)/shard_map/ppermute | solution.py:168
  250.2 1.9 collective-permute-start.19
  252.3 9.1 %collective-permute-done.30 = bf16[1024,256]{0,1:T(8,128)(2,1)S(1)} collective-permute-done((bf16[1024,256]{0,1:T(8,128)(2,1)S(1)}, bf16[1024,256]{0,1:T(8,128)(2,1)S(1)}, u32[]{:S(2)}, u32[]{:S(2)}) %collective-permute-start.30) | collective-permute-done | bytes 524320 | tf_op jit(solution)/shard_map/ppermute | solution.py:168
  261.4 1.9 collective-permute-start.22
  263.6 1.9 collective-permute-start.28
  265.5 7.2 %collective-permute-done.13 = bf16[1024,256]{0,1:T(8,128)(2,1)S(1)} collective-permute-done((bf16[1024,256]{0,1:T(8,128)(2,1)S(1)}, bf16[1024,256]{0,1:T(8,128)(2,1)S(1)}, u32[]{:S(2)}, u32[]{:S(2)}) %collective-permute-start.13) | collective-permute-done | bytes 524320 | tf_op jit(solution)/shard_map/ppermute | solution.py:168
  272.7 1.9 collective-permute-start.25
  274.9 1.9 collective-permute-start.31
  276.8 7.1 %collective-permute-done.19 = bf16[1024,256]{0,1:T(8,128)(2,1)S(1)} collective-permute-done((bf16[1024,256]{0,1:T(8,128)(2,1)S(1)}, bf16[1024,256]{0,1:T(8,128)(2,1)S(1)}, u32[]{:S(2)}, u32[]{:S(2)}) %collective-permute-start.19) | collective-permute-done | bytes 524320 | tf_op jit(solution)/shard_map/ppermute | solution.py:168
  284.2 11.0 %collective-permute-done.25 = bf16[1024,256]{0,1:T(8,128)(2,1)S(1)} collective-permute-done((bf16[1024,256]{0,1:T(8,128)(2,1)S(1)}, bf16[1024,256]{0,1:T(8,128)(2,1)S(1)}, u32[]{:S(2)}, u32[]{:S(2)}) %collective-permute-start.25) | collective-permute-done | bytes 524320 | tf_op jit(solution)/shard_map/ppermute | solution.py:168
  295.4 6.2 %collective-permute-done.31 = bf16[1024,256]{0,1:T(8,128)(2,1)S(1)} collective-permute-done((bf16[1024,256]{0,1:T(8,128)(2,1)S(1)}, bf16[1024,256]{0,1:T(8,128)(2,1)S(1)}, u32[]{:S(2)}, u32[]{:S(2)}) %collective-permute-start.31) | collective-permute-done | bytes 524320 | tf_op jit(solution)/shard_map/ppermute | solution.py:168
  302.1 2.6 copy.9
  (62 shorter events, 11.3 us)
Async XLA Ops:
  3.8 16.4 %collective-permute-start.1 = (bf16[512,1024]{1,0:T(8,128)(2,1)}, bf16[512,1024]{1,0:T(8,128)(2,1)}, u32[]{:S(2)}, u32[]{:S(2)}) collective-permute-start(bf16[512,1024]{1,0:T(8,128)(2,1)} %shard_map.56.refs_2_), channel_id=1, source_target_pairs={{0,4},{4,8},{8,12},{12,16},{16,20},{20,24},{24,28},{1,5},{5,9},{9,... | collective-permute-start | bytes 3145736 | tf_op jit(solution)/shard_map/ppermute | solution.py:21
  9.5 21.8 %collective-permute-start.6 = (bf16[512,1024]{1,0:T(8,128)(2,1)}, bf16[512,1024]{1,0:T(8,128)(2,1)S(1)}, u32[]{:S(2)}, u32[]{:S(2)}) collective-permute-start(bf16[512,1024]{1,0:T(8,128)(2,1)} %shard_map.59.refs_2_), channel_id=1, source_target_pairs={{0,4},{4,8},{8,12},{12,16},{16,20},{20,24},{24,28},{1,5},{5,9},{9,... | collective-permute-start | bytes 3145736 | tf_op jit(solution)/shard_map/ppermute | solution.py:21
  16.9 37.1 %copy-start.3 = (bf16[512,1024]{1,0:T(8,128)(2,1)S(1)}, bf16[512,1024]{1,0:T(8,128)(2,1)}, u32[]{:S(2)}) copy-start(bf16[512,1024]{1,0:T(8,128)(2,1)} %shard_map.56.refs_2_) | copy-start | bytes 3145732
  16.9 25.7 %collective-permute-start.4 = (bf16[512,1024]{1,0:T(8,128)(2,1)}, bf16[512,1024]{1,0:T(8,128)(2,1)S(1)}, u32[]{:S(2)}, u32[]{:S(2)}) collective-permute-start(bf16[512,1024]{1,0:T(8,128)(2,1)} %shard_map.58.refs_2_), channel_id=1, source_target_pairs={{0,4},{4,8},{8,12},{12,16},{16,20},{20,24},{24,28},{1,5},{5,9},{9,... | collective-permute-start | bytes 3145736 | tf_op jit(solution)/shard_map/ppermute | solution.py:21
  20.2 33.7 %collective-permute-start.2 = (bf16[512,1024]{1,0:T(8,128)(2,1)}, bf16[512,1024]{1,0:T(8,128)(2,1)}, u32[]{:S(2)}, u32[]{:S(2)}) collective-permute-start(bf16[512,1024]{1,0:T(8,128)(2,1)} %collective-permute-done.1.refs_1_), channel_id=1, source_target_pairs={{0,4},{4,8},{8,12},{12,16},{16,20},{20,24},{24,28},{1,5},{5,9},{9,... | collective-permute-start | bytes 3145736 | tf_op jit(solution)/shard_map/ppermute | solution.py:21
  26.2 44.0 %collective-permute-start = (bf16[512,1024]{1,0:T(8,128)(2,1)}, bf16[512,1024]{1,0:T(8,128)(2,1)}, u32[]{:S(2)}, u32[]{:S(2)}) collective-permute-start(bf16[512,1024]{1,0:T(8,128)(2,1)} %shard_map.55.refs_2_), channel_id=1, source_target_pairs={{0,4},{4,8},{8,12},{12,16},{16,20},{20,24},{24,28},{1,5},{5,9},{9,... | collective-permute-start | bytes 3145736 | tf_op jit(solution)/shard_map/ppermute | solution.py:21
  30.4 45.9 %copy-start.1 = (bf16[512,1024]{1,0:T(8,128)(2,1)S(1)}, bf16[512,1024]{1,0:T(8,128)(2,1)}, u32[]{:S(2)}) copy-start(bf16[512,1024]{1,0:T(8,128)(2,1)} %shard_map.59.refs_2_) | copy-start | bytes 3145732
  31.4 44.9 %collective-permute-start.7 = (bf16[512,1024]{1,0:T(8,128)(2,1)S(1)}, bf16[512,1024]{1,0:T(8,128)(2,1)S(1)}, u32[]{:S(2)}, u32[]{:S(2)}) collective-permute-start(bf16[512,1024]{1,0:T(8,128)(2,1)S(1)} %collective-permute-done.6.refs_1_), channel_id=1, source_target_pairs={{0,4},{4,8},{8,12},{12,16},{16,20},{20,24},{24,28},{1,5},{5,9},{9,... | collective-permute-start | bytes 3145736 | tf_op jit(solution)/shard_map/ppermute | solution.py:21
  42.6 45.6 %collective-permute-start.5 = (bf16[512,1024]{1,0:T(8,128)(2,1)S(1)}, bf16[512,1024]{1,0:T(8,128)(2,1)S(1)}, u32[]{:S(2)}, u32[]{:S(2)}) collective-permute-start(bf16[512,1024]{1,0:T(8,128)(2,1)S(1)} %collective-permute-done.4.refs_1_), channel_id=1, source_target_pairs={{0,4},{4,8},{8,12},{12,16},{16,20},{20,24},{24,28},{1,5},{5,9},{9,... | collective-permute-start | bytes 3145736 | tf_op jit(solution)/shard_map/ppermute | solution.py:21
  53.9 2.2 copy-start.4
  56.1 1.0 copy-start.6
  57.2 19.1 %copy-start.5 = (bf16[1024,2048]{1,0:T(8,128)(2,1)S(1)}, bf16[1024,2048]{1,0:T(8,128)(2,1)}, u32[]{:S(2)}) copy-start(bf16[1024,2048]{1,0:T(8,128)(2,1)} %gate_ref.7) | copy-start | bytes 12582916
  70.2 18.0 %copy-start = (bf16[512,1024]{1,0:T(8,128)(2,1)S(1)}, bf16[512,1024]{1,0:T(8,128)(2,1)}, u32[]{:S(2)}) copy-start(bf16[512,1024]{1,0:T(8,128)(2,1)} %shard_map.58.refs_2_) | copy-start | bytes 3145732
  70.3 29.9 %collective-permute-start.3 = (bf16[512,1024]{1,0:T(8,128)(2,1)}, bf16[512,1024]{1,0:T(8,128)(2,1)S(1)}, u32[]{:S(2)}, u32[]{:S(2)}) collective-permute-start(bf16[512,1024]{1,0:T(8,128)(2,1)} %collective-permute-done.refs_1_), channel_id=1, source_target_pairs={{0,4},{4,8},{8,12},{12,16},{16,20},{20,24},{24,28},{1,5},{5,9},{9,... | collective-permute-start | bytes 3145736 | tf_op jit(solution)/shard_map/ppermute | solution.py:21
  88.2 12.0 %copy-start.2 = (bf16[512,1024]{1,0:T(8,128)(2,1)S(1)}, bf16[512,1024]{1,0:T(8,128)(2,1)}, u32[]{:S(2)}) copy-start(bf16[512,1024]{1,0:T(8,128)(2,1)} %shard_map.55.refs_2_) | copy-start | bytes 3145732
  113.0 2.0 copy-start.7
  125.7 2.4 copy-start.11
  126.8 44.0 %collective-permute-start.8 = (bf16[1024,256]{0,1:T(8,128)(2,1)}, bf16[1024,256]{0,1:T(8,128)(2,1)S(1)}, u32[]{:S(2)}, u32[]{:S(2)}) collective-permute-start(bf16[1024,256]{0,1:T(8,128)(2,1)} %get-tuple-element.25), channel_id=1, source_target_pairs={{0,1},{4,5},{8,9},{12,13},{16,17},{20,21},{24,25},{28,29}} | collective-permute-start | bytes 1572872 | tf_op jit(solution)/shard_map/ppermute | solution.py:165
  128.1 62.5 %collective-permute-start.11 = (bf16[1024,256]{0,1:T(8,128)(2,1)}, bf16[1024,256]{0,1:T(8,128)(2,1)}, u32[]{:S(2)}, u32[]{:S(2)}) collective-permute-start(bf16[1024,256]{0,1:T(8,128)(2,1)} %get-tuple-element.26), channel_id=1, source_target_pairs={{3,2},{7,6},{11,10},{15,14},{19,18},{23,22},{27,26},{31,30}} | collective-permute-start | bytes 1572872 | tf_op jit(solution)/shard_map/ppermute | solution.py:168
  140.3 15.9 %copy-start.8 = (bf16[4096,256]{0,1:T(8,128)(2,1)}, bf16[4096,256]{0,1:T(8,128)(2,1)S(1)}, u32[]{:S(2)}) copy-start(bf16[4096,256]{0,1:T(8,128)(2,1)S(1)} %fusion.1) | copy-start | bytes 6291460
  141.5 32.2 %collective-permute-start.14 = (bf16[1024,256]{0,1:T(8,128)(2,1)}, bf16[1024,256]{0,1:T(8,128)(2,1)S(1)}, u32[]{:S(2)}, u32[]{:S(2)}) collective-permute-start(bf16[1024,256]{0,1:T(8,128)(2,1)} %get-tuple-element.29), channel_id=1, source_target_pairs={{0,1},{4,5},{8,9},{12,13},{16,17},{20,21},{24,25},{28,29}} | collective-permute-start | bytes 1572872 | tf_op jit(solution)/shard_map/ppermute | solution.py:165
  142.7 60.4 %collective-permute-start.17 = (bf16[1024,256]{0,1:T(8,128)(2,1)}, bf16[1024,256]{0,1:T(8,128)(2,1)}, u32[]{:S(2)}, u32[]{:S(2)}) collective-permute-start(bf16[1024,256]{0,1:T(8,128)(2,1)} %get-tuple-element.30), channel_id=1, source_target_pairs={{3,2},{7,6},{11,10},{15,14},{19,18},{23,22},{27,26},{31,30}} | collective-permute-start | bytes 1572872 | tf_op jit(solution)/shard_map/ppermute | solution.py:168
  158.5 18.5 %collective-permute-start.20 = (bf16[1024,256]{0,1:T(8,128)(2,1)}, bf16[1024,256]{0,1:T(8,128)(2,1)}, u32[]{:S(2)}, u32[]{:S(2)}) collective-permute-start(bf16[1024,256]{0,1:T(8,128)(2,1)} %get-tuple-element.33), channel_id=1, source_target_pairs={{0,1},{4,5},{8,9},{12,13},{16,17},{20,21},{24,25},{28,29}} | collective-permute-start | bytes 1572872 | tf_op jit(solution)/shard_map/ppermute | solution.py:165
  170.7 6.3 %copy-start.13 = (bf16[1024,256]{0,1:T(8,128)(2,1)S(1)}, bf16[1024,256]{0,1:T(8,128)(2,1)}, u32[]{:S(2)}) copy-start(bf16[1024,256]{0,1:T(8,128)(2,1)} %get-tuple-element.34) | copy-start | bytes 1572868
  170.8 7.0 %copy-start.10 = (bf16[4096,256]{0,1:T(8,128)(2,1)S(1)}, bf16[4096,256]{0,1:T(8,128)(2,1)}, u32[]{:S(2)}) copy-start(bf16[4096,256]{0,1:T(8,128)(2,1)} %fusion.2) | copy-start | bytes 6291460
  170.8 30.9 %copy-start.12 = (bf16[4096,256]{0,1:T(8,128)(2,1)S(1)}, bf16[4096,256]{0,1:T(8,128)(2,1)}, u32[]{:S(2)}) copy-start(bf16[4096,256]{0,1:T(8,128)(2,1)} %copy-done.11) | copy-start | bytes 6291460
  170.9 17.7 %collective-permute-start.26 = (bf16[1024,256]{0,1:T(8,128)(2,1)S(1)}, bf16[1024,256]{0,1:T(8,128)(2,1)S(1)}, u32[]{:S(2)}, u32[]{:S(2)}) collective-permute-start(bf16[1024,256]{0,1:T(8,128)(2,1)S(1)} %get-tuple-element.37), channel_id=1, source_target_pairs={{0,1},{4,5},{8,9},{12,13},{16,17},{20,21},{24,25},{28,29}} | collective-permute-start | bytes 1572872 | tf_op jit(solution)/shard_map/ppermute | solution.py:165
  173.7 38.6 %copy-start.9 = (bf16[4096,256]{0,1:T(8,128)(2,1)S(1)}, bf16[4096,256]{0,1:T(8,128)(2,1)}, u32[]{:S(2)}) copy-start(bf16[4096,256]{0,1:T(8,128)(2,1)} %copy-done.8) | copy-start | bytes 6291460
  173.7 26.1 %collective-permute-start.9 = (bf16[1024,256]{0,1:T(8,128)(2,1)S(1)}, bf16[1024,256]{0,1:T(8,128)(2,1)S(1)}, u32[]{:S(2)}, u32[]{:S(2)}) collective-permute-start(bf16[1024,256]{0,1:T(8,128)(2,1)S(1)} %add_convert_fusion.19), channel_id=1, source_target_pairs={{0,1},{1,2},{4,5},{5,6},{8,9},{9,10},{12,13},{13,14},{16,17},{17,1... | collective-permute-start | bytes 1572872 | tf_op jit(solution)/shard_map/ppermute | solution.py:165
  177.0 36.7 %collective-permute-start.23 = (bf16[1024,256]{0,1:T(8,128)(2,1)S(1)}, bf16[1024,256]{0,1:T(8,128)(2,1)S(1)}, u32[]{:S(2)}, u32[]{:S(2)}) collective-permute-start(bf16[1024,256]{0,1:T(8,128)(2,1)S(1)} %copy-done.13), channel_id=1, source_target_pairs={{3,2},{7,6},{11,10},{15,14},{19,18},{23,22},{27,26},{31,30}} | collective-permute-start | bytes 1572872 | tf_op jit(solution)/shard_map/ppermute | solution.py:168
  188.5 22.5 %collective-permute-start.15 = (bf16[1024,256]{0,1:T(8,128)(2,1)S(1)}, bf16[1024,256]{0,1:T(8,128)(2,1)S(1)}, u32[]{:S(2)}, u32[]{:S(2)}) collective-permute-start(bf16[1024,256]{0,1:T(8,128)(2,1)S(1)} %add_convert_fusion.14), channel_id=1, source_target_pairs={{0,1},{1,2},{4,5},{5,6},{8,9},{9,10},{12,13},{13,14},{16,17},{17,1... | collective-permute-start | bytes 1572872 | tf_op jit(solution)/shard_map/ppermute | solution.py:165
  190.7 33.3 %collective-permute-start.29 = (bf16[1024,256]{0,1:T(8,128)(2,1)S(1)}, bf16[1024,256]{0,1:T(8,128)(2,1)S(1)}, u32[]{:S(2)}, u32[]{:S(2)}) collective-permute-start(bf16[1024,256]{0,1:T(8,128)(2,1)S(1)} %get-tuple-element.38), channel_id=1, source_target_pairs={{3,2},{7,6},{11,10},{15,14},{19,18},{23,22},{27,26},{31,30}} | collective-permute-start | bytes 1572872 | tf_op jit(solution)/shard_map/ppermute | solution.py:168
  199.8 22.5 %collective-permute-start.21 = (bf16[1024,256]{0,1:T(8,128)(2,1)S(1)}, bf16[1024,256]{0,1:T(8,128)(2,1)S(1)}, u32[]{:S(2)}, u32[]{:S(2)}) collective-permute-start(bf16[1024,256]{0,1:T(8,128)(2,1)S(1)} %add_convert_fusion.9), channel_id=1, source_target_pairs={{0,1},{1,2},{4,5},{5,6},{8,9},{9,10},{12,13},{13,14},{16,17},{17,1... | collective-permute-start | bytes 1572872 | tf_op jit(solution)/shard_map/ppermute | solution.py:165
  203.1 30.3 %collective-permute-start.27 = (bf16[1024,256]{0,1:T(8,128)(2,1)S(1)}, bf16[1024,256]{0,1:T(8,128)(2,1)S(1)}, u32[]{:S(2)}, u32[]{:S(2)}) collective-permute-start(bf16[1024,256]{0,1:T(8,128)(2,1)S(1)} %add_convert_fusion.4), channel_id=1, source_target_pairs={{0,1},{1,2},{4,5},{5,6},{8,9},{9,10},{12,13},{13,14},{16,17},{17,1... | collective-permute-start | bytes 1572872 | tf_op jit(solution)/shard_map/ppermute | solution.py:165
  211.0 24.1 %collective-permute-start.12 = (bf16[1024,256]{0,1:T(8,128)(2,1)S(1)}, bf16[1024,256]{0,1:T(8,128)(2,1)S(1)}, u32[]{:S(2)}, u32[]{:S(2)}) collective-permute-start(bf16[1024,256]{0,1:T(8,128)(2,1)S(1)} %get-tuple-element.40), channel_id=1, source_target_pairs={{3,2},{2,1},{7,6},{6,5},{11,10},{10,9},{15,14},{14,13},{19,18},{18... | collective-permute-start | bytes 1572872 | tf_op jit(solution)/shard_map/ppermute | solution.py:168
  213.8 49.8 %collective-permute-start.10 = (bf16[1024,256]{0,1:T(8,128)(2,1)S(1)}, bf16[1024,256]{0,1:T(8,128)(2,1)S(1)}, u32[]{:S(2)}, u32[]{:S(2)}) collective-permute-start(bf16[1024,256]{0,1:T(8,128)(2,1)S(1)} %get-tuple-element.39), channel_id=1, source_target_pairs={{0,1},{1,2},{2,3},{4,5},{5,6},{6,7},{8,9},{9,10},{10,11},{12,13},{... | collective-permute-start | bytes 1572872 | tf_op jit(solution)/shard_map/ppermute | solution.py:165
  222.2 14.4 %collective-permute-start.18 = (bf16[1024,256]{0,1:T(8,128)(2,1)S(1)}, bf16[1024,256]{0,1:T(8,128)(2,1)S(1)}, u32[]{:S(2)}, u32[]{:S(2)}) collective-permute-start(bf16[1024,256]{0,1:T(8,128)(2,1)S(1)} %get-tuple-element.42), channel_id=1, source_target_pairs={{3,2},{2,1},{7,6},{6,5},{11,10},{10,9},{15,14},{14,13},{19,18},{18... | collective-permute-start | bytes 1572872 | tf_op jit(solution)/shard_map/ppermute | solution.py:168
  224.0 50.9 %collective-permute-start.16 = (bf16[1024,256]{0,1:T(8,128)(2,1)S(1)}, bf16[1024,256]{0,1:T(8,128)(2,1)S(1)}, u32[]{:S(2)}, u32[]{:S(2)}) collective-permute-start(bf16[1024,256]{0,1:T(8,128)(2,1)S(1)} %get-tuple-element.41), channel_id=1, source_target_pairs={{0,1},{1,2},{2,3},{4,5},{5,6},{6,7},{8,9},{9,10},{10,11},{12,13},{... | collective-permute-start | bytes 1572872 | tf_op jit(solution)/shard_map/ppermute | solution.py:165
  233.5 16.7 %collective-permute-start.24 = (bf16[1024,256]{0,1:T(8,128)(2,1)S(1)}, bf16[1024,256]{0,1:T(8,128)(2,1)S(1)}, u32[]{:S(2)}, u32[]{:S(2)}) collective-permute-start(bf16[1024,256]{0,1:T(8,128)(2,1)S(1)} %get-tuple-element.44), channel_id=1, source_target_pairs={{3,2},{2,1},{7,6},{6,5},{11,10},{10,9},{15,14},{14,13},{19,18},{18... | collective-permute-start | bytes 1572872 | tf_op jit(solution)/shard_map/ppermute | solution.py:168
  235.2 26.3 %collective-permute-start.30 = (bf16[1024,256]{0,1:T(8,128)(2,1)S(1)}, bf16[1024,256]{0,1:T(8,128)(2,1)S(1)}, u32[]{:S(2)}, u32[]{:S(2)}) collective-permute-start(bf16[1024,256]{0,1:T(8,128)(2,1)S(1)} %get-tuple-element.46), channel_id=1, source_target_pairs={{3,2},{2,1},{7,6},{6,5},{11,10},{10,9},{15,14},{14,13},{19,18},{18... | collective-permute-start | bytes 1572872 | tf_op jit(solution)/shard_map/ppermute | solution.py:168
  236.7 36.0 %collective-permute-start.13 = (bf16[1024,256]{0,1:T(8,128)(2,1)S(1)}, bf16[1024,256]{0,1:T(8,128)(2,1)S(1)}, u32[]{:S(2)}, u32[]{:S(2)}) collective-permute-start(bf16[1024,256]{0,1:T(8,128)(2,1)S(1)} %add_convert_fusion.16), channel_id=1, source_target_pairs={{3,2},{2,1},{1,0},{7,6},{6,5},{5,4},{11,10},{10,9},{9,8},{15,14},{... | collective-permute-start | bytes 1572872 | tf_op jit(solution)/shard_map/ppermute | solution.py:168
  250.2 33.7 %collective-permute-start.19 = (bf16[1024,256]{0,1:T(8,128)(2,1)S(1)}, bf16[1024,256]{0,1:T(8,128)(2,1)S(1)}, u32[]{:S(2)}, u32[]{:S(2)}) collective-permute-start(bf16[1024,256]{0,1:T(8,128)(2,1)S(1)} %add_convert_fusion.11), channel_id=1, source_target_pairs={{3,2},{2,1},{1,0},{7,6},{6,5},{5,4},{11,10},{10,9},{9,8},{15,14},{... | collective-permute-start | bytes 1572872 | tf_op jit(solution)/shard_map/ppermute | solution.py:168
  261.4 22.7 %collective-permute-start.22 = (bf16[1024,256]{0,1:T(8,128)(2,1)S(1)}, bf16[1024,256]{0,1:T(8,128)(2,1)S(1)}, u32[]{:S(2)}, u32[]{:S(2)}) collective-permute-start(bf16[1024,256]{0,1:T(8,128)(2,1)S(1)} %get-tuple-element.43), channel_id=1, source_target_pairs={{0,1},{1,2},{2,3},{4,5},{5,6},{6,7},{8,9},{9,10},{10,11},{12,13},{... | collective-permute-start | bytes 1572872 | tf_op jit(solution)/shard_map/ppermute | solution.py:165
  263.6 31.8 %collective-permute-start.28 = (bf16[1024,256]{0,1:T(8,128)(2,1)S(1)}, bf16[1024,256]{0,1:T(8,128)(2,1)S(1)}, u32[]{:S(2)}, u32[]{:S(2)}) collective-permute-start(bf16[1024,256]{0,1:T(8,128)(2,1)S(1)} %get-tuple-element.45), channel_id=1, source_target_pairs={{0,1},{1,2},{2,3},{4,5},{5,6},{6,7},{8,9},{9,10},{10,11},{12,13},{... | collective-permute-start | bytes 1572872 | tf_op jit(solution)/shard_map/ppermute | solution.py:165
  272.7 22.5 %collective-permute-start.25 = (bf16[1024,256]{0,1:T(8,128)(2,1)S(1)}, bf16[1024,256]{0,1:T(8,128)(2,1)S(1)}, u32[]{:S(2)}, u32[]{:S(2)}) collective-permute-start(bf16[1024,256]{0,1:T(8,128)(2,1)S(1)} %add_convert_fusion.6), channel_id=1, source_target_pairs={{3,2},{2,1},{1,0},{7,6},{6,5},{5,4},{11,10},{10,9},{9,8},{15,14},{... | collective-permute-start | bytes 1572872 | tf_op jit(solution)/shard_map/ppermute | solution.py:168
  274.9 26.8 %collective-permute-start.31 = (bf16[1024,256]{0,1:T(8,128)(2,1)S(1)}, bf16[1024,256]{0,1:T(8,128)(2,1)S(1)}, u32[]{:S(2)}, u32[]{:S(2)}) collective-permute-start(bf16[1024,256]{0,1:T(8,128)(2,1)S(1)} %add_convert_fusion.1), channel_id=1, source_target_pairs={{3,2},{2,1},{1,0},{7,6},{6,5},{5,4},{11,10},{10,9},{9,8},{15,14},{... | collective-permute-start | bytes 1572872 | tf_op jit(solution)/shard_map/ppermute | solution.py:168
